TPU v7x, 32 devices: a whole 2x2x4 slice. The times are simulated.
32 devices in a mesh: ctx: 8 (over z, y), head: 4 (over x, core).
Axes of the slice: x: 2, y: 2, z: 4, core: 2. Of those that a mesh axis runs over, the one named last changes fastest.
Arguments:
- queries: bfloat16 [2048, 4096], P(('ctx', 'head')), may hold values from -6 to 6
- key_rows: bfloat16 [2048, 512], P(('ctx', 'head')), may hold values from -6 to 6
- value_rows: bfloat16 [2048, 512], P(('ctx', 'head')), may hold values from -6 to 6
- attn_out: bfloat16 [2048, 4096], P(('ctx', 'head')), may hold values from -6 to 6
- out_grad: bfloat16 [2048, 4096], P(('ctx', 'head')), may hold values from -864 to 864
- logsumexp: float32 [32, 2048], P('head', 'ctx'), may hold values from 7.5 to 8.7
Outputs:
- grad_queries: float32 [2048, 4096], P(('ctx', 'head'))
- grad_keys: float32 [2048, 512], P(('ctx', 'head'))
- grad_values: float32 [2048, 512], P(('ctx', 'head'))
All inputs are finite; a program needn't handle non-finite values.
Results may differ from a plain program's by a relative error of at most 0.0051.
Values may be sent and summed in bfloat16 or wider, within the bound.
No kernel may reach another device: no remote copies, remote signals or barrier semaphores. Data moves between devices by JAX's collectives and lax.ppermute only.
A program may use at most 64 MiB of HBM per device.

v0:
```python
import math
import jax
import jax.numpy as jnp
from jax import lax
from jax.sharding import PartitionSpec as P

HEAD_DIM = 128
GROUP = 8
BLOCK = 256


def from_partner(value, axis, distance):
    return lax.ppermute(value, axis, [(i, i ^ 1 << distance) for i in range(lax.axis_size(axis))])


def block_grads(query_blk, grad_blk, lse_rows, dot_rows, key_blk, value_blk):
    score_scale = 1.0 / math.sqrt(query_blk.shape[-1])
    scores = (
        jnp.einsum("nbhgd,nkhd->nhgbk", query_blk, key_blk, preferred_element_type=jnp.float32)
        * score_scale
    )
    attn_probs = jnp.exp(scores - lse_rows[..., None])
    dprobs = jnp.einsum(
        "nbhgd,nkhd->nhgbk", grad_blk, value_blk, preferred_element_type=jnp.float32
    )
    dscores = (attn_probs * (dprobs - dot_rows[..., None])).astype(jnp.bfloat16)
    weights = attn_probs.astype(jnp.bfloat16)
    d_values = jnp.einsum(
        "nhgbk,nbhgd->nkhd", weights, grad_blk, preferred_element_type=jnp.float32
    )
    d_query = (
        jnp.einsum("nhgbk,nkhd->nbhgd", dscores, key_blk, preferred_element_type=jnp.float32)
        * score_scale
    )
    d_keys = (
        jnp.einsum("nhgbk,nbhgd->nkhd", dscores, query_blk, preferred_element_type=jnp.float32)
        * score_scale
    )
    return (d_query, d_keys, d_values)


def on_device(queries, key_rows, value_rows, attn_out, out_grad, logsumexp):
    rows_before = queries.shape[0]
    dot_before = jnp.sum(
        (out_grad.astype(jnp.float32) * attn_out.astype(jnp.float32)).reshape(
            rows_before, -1, HEAD_DIM
        ),
        axis=2,
    )
    q_local, k_local, v_local, g_local = (
        lax.all_to_all(queries, "head", split_axis=1, concat_axis=0, tiled=True),
        lax.all_to_all(key_rows, "head", split_axis=1, concat_axis=0, tiled=True),
        lax.all_to_all(value_rows, "head", split_axis=1, concat_axis=0, tiled=True),
        lax.all_to_all(out_grad, "head", split_axis=1, concat_axis=0, tiled=True),
    )
    dot_local = lax.all_to_all(dot_before, "head", split_axis=1, concat_axis=0, tiled=True)
    row_count = q_local.shape[0]
    blocks = row_count // BLOCK
    kv_heads = k_local.shape[1] // HEAD_DIM
    query_blk = q_local.reshape(blocks, BLOCK, kv_heads, GROUP, HEAD_DIM)
    grad_blk = g_local.reshape(blocks, BLOCK, kv_heads, GROUP, HEAD_DIM)
    key_blk = k_local.reshape(blocks, BLOCK, kv_heads, HEAD_DIM)
    value_blk = v_local.reshape(blocks, BLOCK, kv_heads, HEAD_DIM)
    lse_rows = logsumexp.reshape(kv_heads, GROUP, blocks, BLOCK).transpose(2, 0, 1, 3)
    dot_rows = dot_local.reshape(blocks, BLOCK, kv_heads, GROUP).transpose(0, 2, 3, 1)
    grad_q, grad_k, grad_v = block_grads(
        query_blk, grad_blk, lse_rows, dot_rows, key_blk, value_blk
    )
    ctx_levels = lax.axis_size("ctx").bit_length() - 1
    plan = list(range(ctx_levels))
    for bit_level in plan:
        far_k, far_v = from_partner((key_blk, value_blk), "ctx", bit_level)
        part_q, part_k, part_v = block_grads(query_blk, grad_blk, lse_rows, dot_rows, far_k, far_v)
        back_k, back_v = from_partner((part_k, part_v), "ctx", bit_level)
        grad_q = grad_q + part_q
        grad_k = grad_k + back_k
        grad_v = grad_v + back_v
    result_q, result_k, result_v = (
        lax.all_to_all(
            grad_q.reshape(row_count, -1), "head", split_axis=0, concat_axis=1, tiled=True
        ),
        lax.all_to_all(
            grad_k.reshape(row_count, -1), "head", split_axis=0, concat_axis=1, tiled=True
        ),
        lax.all_to_all(
            grad_v.reshape(row_count, -1), "head", split_axis=0, concat_axis=1, tiled=True
        ),
    )
    return (result_q, result_k, result_v)


def solution(mesh):
    placed = (
        P(("ctx", "head"), None),
        P(("ctx", "head"), None),
        P(("ctx", "head"), None),
        P(("ctx", "head"), None),
        P(("ctx", "head"), None),
        P("head", "ctx"),
    )
    return jax.shard_map(
        on_device,
        mesh=mesh,
        in_specs=placed,
        out_specs=(P(("ctx", "head"), None), P(("ctx", "head"), None), P(("ctx", "head"), None)),
        check_vma=False,
    )
```

profile of v0, /device:TPU:0, one launch (start us, length us, event | category | flops | bytes accessed | tf_op | source)
XLA Modules:
  0.0 108.8 jit_solution(2686458098232040991)
XLA Ops:
  3.3 4.2 %all-to-all-start.4 = ((f32[4,1,512]{2,1,0:T(1,128)}), f32[4,1,512]{2,1,0:T(1,128)S(1)}, u32[]{:S(2)}, u32[]{:S(2)}) async-start(f32[4,1,512]{2,1,0:T(1,128)} %reshape.241), calls=%async_computation.4 | async-start | bytes 16384 | tf_op jit(solution)/shard_map/all_to_all | solution.py:56
  8.2 3.2 %all-to-all-done.4 = f32[4,1,512]{2,1,0:T(1,128)S(1)} async-done(((f32[4,1,512]{2,1,0:T(1,128)}), f32[4,1,512]{2,1,0:T(1,128)S(1)}, u32[]{:S(2)}, u32[]{:S(2)}) %all-to-all-start.4) | async-done | bytes 8224 | tf_op jit(solution)/shard_map/all_to_all | solution.py:56
  11.4 3.3 %all-to-all-start = ((bf16[64,4,128]{2,0,1:T(8,128)(2,1)}), bf16[64,4,128]{2,0,1:T(8,128)(2,1)S(1)}, u32[]{:S(2)}, u32[]{:S(2)}) async-start(bf16[64,4,128]{2,0,1:T(8,128)(2,1)} %copy_bitcast_fusion.5), calls=%async_computation | async-start | bytes 131072 | tf_op jit(solution)/shard_map/all_to_all | solution.py:52
  15.3 3.4 %all-to-all-done = bf16[64,4,128]{2,0,1:T(8,128)(2,1)S(1)} async-done(((bf16[64,4,128]{2,0,1:T(8,128)(2,1)}), bf16[64,4,128]{2,0,1:T(8,128)(2,1)S(1)}, u32[]{:S(2)}, u32[]{:S(2)}) %all-to-all-start) | async-done | bytes 65568 | tf_op jit(solution)/shard_map/all_to_all | solution.py:52
  18.8 3.3 %all-to-all-start.2 = ((bf16[64,4,128]{2,0,1:T(8,128)(2,1)}), bf16[64,4,128]{2,0,1:T(8,128)(2,1)S(1)}, u32[]{:S(2)}, u32[]{:S(2)}) async-start(bf16[64,4,128]{2,0,1:T(8,128)(2,1)} %copy_bitcast_fusion.4), calls=%async_computation.2 | async-start | bytes 131072 | tf_op jit(solution)/shard_map/all_to_all | solution.py:53
  22.9 3.2 %all-to-all-done.2 = bf16[64,4,128]{2,0,1:T(8,128)(2,1)S(1)} async-done(((bf16[64,4,128]{2,0,1:T(8,128)(2,1)}), bf16[64,4,128]{2,0,1:T(8,128)(2,1)S(1)}, u32[]{:S(2)}, u32[]{:S(2)}) %all-to-all-start.2) | async-done | bytes 65568 | tf_op jit(solution)/shard_map/all_to_all | solution.py:53
  26.1 3.5 %all-to-all-start.1 = ((bf16[64,4,1024]{2,0,1:T(8,128)(2,1)}), bf16[64,4,1024]{2,0,1:T(8,128)(2,1)S(1)}, u32[]{:S(2)}, u32[]{:S(2)}) async-start(bf16[64,4,1024]{2,0,1:T(8,128)(2,1)} %bitcast.347), calls=%async_computation.1 | async-start | bytes 1048576 | tf_op jit(solution)/shard_map/all_to_all | solution.py:51
  30.5 7.9 %all-to-all-done.1 = bf16[64,4,1024]{2,0,1:T(8,128)(2,1)S(1)} async-done(((bf16[64,4,1024]{2,0,1:T(8,128)(2,1)}), bf16[64,4,1024]{2,0,1:T(8,128)(2,1)S(1)}, u32[]{:S(2)}, u32[]{:S(2)}) %all-to-all-start.1) | async-done | bytes 524320 | tf_op jit(solution)/shard_map/all_to_all | solution.py:51
  38.4 3.5 %all-to-all-start.3 = ((bf16[64,4,1024]{2,0,1:T(8,128)(2,1)}), bf16[64,4,1024]{2,0,1:T(8,128)(2,1)S(1)}, u32[]{:S(2)}, u32[]{:S(2)}) async-start(bf16[64,4,1024]{2,0,1:T(8,128)(2,1)} %bitcast.346), calls=%async_computation.3 | async-start | bytes 1048576 | tf_op jit(solution)/shard_map/all_to_all | solution.py:54
  43.1 2.0 %collective-permute-start = (bf16[1,256,1,128]{3,1,2,0:T(8,128)(2,1)S(1)}, bf16[1,256,1,128]{3,1,2,0:T(8,128)(2,1)S(1)}, u32[]{:S(2)}, u32[]{:S(2)}) collective-permute-start(bf16[1,256,1,128]{3,1,2,0:T(8,128)(2,1)S(1)} %bitcast.370), channel_id=1, source_target_pairs={{0,4},{4,0},{8,12},{12,8},{16,20},{20,16},{24,28},{28,24},{1,5},{5... | collective-permute-start | bytes 196616 | tf_op jit(solution)/shard_map/ppermute | solution.py:13
  45.2 2.6 %collective-permute-start.5 = (bf16[1,256,1,128]{3,1,2,0:T(8,128)(2,1)S(1)}, bf16[1,256,1,128]{3,1,2,0:T(8,128)(2,1)S(1)}, u32[]{:S(2)}, u32[]{:S(2)}) collective-permute-start(bf16[1,256,1,128]{3,1,2,0:T(8,128)(2,1)S(1)} %bitcast.376), channel_id=1, source_target_pairs={{0,16},{4,20},{8,24},{12,28},{16,0},{20,4},{24,8},{28,12},{1,17},{... | collective-permute-start | bytes 196616 | tf_op jit(solution)/shard_map/ppermute | solution.py:13
  47.8 1.6 %collective-permute-start.3 = (bf16[1,256,1,128]{3,1,2,0:T(8,128)(2,1)S(1)}, bf16[1,256,1,128]{3,1,2,0:T(8,128)(2,1)S(1)}, u32[]{:S(2)}, u32[]{:S(2)}) collective-permute-start(bf16[1,256,1,128]{3,1,2,0:T(8,128)(2,1)S(1)} %bitcast.377), channel_id=1, source_target_pairs={{0,8},{4,12},{8,0},{12,4},{16,24},{20,28},{24,16},{28,20},{1,9},{5... | collective-permute-start | bytes 196616 | tf_op jit(solution)/shard_map/ppermute | solution.py:13
  50.8 2.1 %collective-permute-start.2 = (bf16[1,256,1,128]{3,1,2,0:T(8,128)(2,1)S(1)}, bf16[1,256,1,128]{3,1,2,0:T(8,128)(2,1)S(1)}, u32[]{:S(2)}, u32[]{:S(2)}) collective-permute-start(bf16[1,256,1,128]{3,1,2,0:T(8,128)(2,1)S(1)} %bitcast.372), channel_id=1, source_target_pairs={{0,8},{4,12},{8,0},{12,4},{16,24},{20,28},{24,16},{28,20},{1,9},{5... | collective-permute-start | bytes 196616 | tf_op jit(solution)/shard_map/ppermute | solution.py:13
  55.0 1.6 %collective-permute-start.6 = (f32[1,256,1,128]{3,1,2,0:T(8,128)S(1)}, f32[1,256,1,128]{3,1,2,0:T(8,128)S(1)}, u32[]{:S(2)}, u32[]{:S(2)}) collective-permute-start(f32[1,256,1,128]{3,1,2,0:T(8,128)S(1)} %fusion.28), channel_id=1, source_target_pairs={{0,4},{4,0},{8,12},{12,8},{16,20},{20,16},{24,28},{28,24},{1,5},{5... | collective-permute-start | bytes 393224 | tf_op jit(solution)/shard_map/ppermute | solution.py:13
  61.4 1.6 %collective-permute-start.9 = (f32[1,256,1,128]{3,1,2,0:T(8,128)S(1)}, f32[1,256,1,128]{3,1,2,0:T(8,128)S(1)}, u32[]{:S(2)}, u32[]{:S(2)}) collective-permute-start(f32[1,256,1,128]{3,1,2,0:T(8,128)S(1)} %convolution_bitcast_fusion.2), channel_id=1, source_target_pairs={{0,4},{4,0},{8,12},{12,8},{16,20},{20,16},{24,28},{28,24},{1,5},{5... | collective-permute-start | bytes 393224 | tf_op jit(solution)/shard_map/ppermute | solution.py:13
  65.1 2.0 %collective-permute-start.11 = (f32[1,256,1,128]{3,1,2,0:T(8,128)S(1)}, f32[1,256,1,128]{3,1,2,0:T(8,128)S(1)}, u32[]{:S(2)}, u32[]{:S(2)}) collective-permute-start(f32[1,256,1,128]{3,1,2,0:T(8,128)S(1)} %convolution_bitcast_fusion), channel_id=1, source_target_pairs={{0,16},{4,20},{8,24},{12,28},{16,0},{20,4},{24,8},{28,12},{1,17},{... | collective-permute-start | bytes 393224 | tf_op jit(solution)/shard_map/ppermute | solution.py:13
  69.2 1.5 %convolution_add_fusion.1 = f32[8,256,128]{2,1,0:T(8,128)} fusion(f32[8,256,128]{2,1,0:T(8,128)S(1)} %fusion.87, bf16[8,256,256]{1,2,0:T(8,128)(2,1)S(1)} %fusion.17, bf16[1,256,1,128]{3,1,2,0:T(8,128)(2,1)S(1)} %collective-permute-done), kind=kOutput, calls=%fused_computation.30 | convolution fusion | flops 134479872 | bytes 3211264 | tf_op jit(solution)/shard_map/nhgbk,nkhd->nbhgd/dot_general | solution.py:32
  74.0 3.3 %all-to-all-start.7 = ((f32[4,64,128]{2,1,0:T(8,128)}), f32[4,64,128]{2,1,0:T(8,128)S(1)}, u32[]{:S(2)}, u32[]{:S(2)}) async-start(f32[4,64,128]{2,1,0:T(8,128)} %bitcast.90), calls=%async_computation.7 | async-start | bytes 262144 | tf_op jit(solution)/shard_map/all_to_all | solution.py:85
  77.4 1.9 %collective-permute-done.8 = f32[1,256,1,128]{3,1,2,0:T(8,128)S(1)} collective-permute-done((f32[1,256,1,128]{3,1,2,0:T(8,128)}, f32[1,256,1,128]{3,1,2,0:T(8,128)S(1)}, u32[]{:S(2)}, u32[]{:S(2)}) %collective-permute-start.8) | collective-permute-done | bytes 131104 | tf_op jit(solution)/shard_map/ppermute | solution.py:13
  80.4 1.6 %all-to-all-done.7 = f32[4,64,128]{2,1,0:T(8,128)S(1)} async-done(((f32[4,64,128]{2,1,0:T(8,128)}), f32[4,64,128]{2,1,0:T(8,128)S(1)}, u32[]{:S(2)}, u32[]{:S(2)}) %all-to-all-start.7) | async-done | bytes 131104 | tf_op jit(solution)/shard_map/all_to_all | solution.py:85
  81.9 3.3 %all-to-all-start.6 = ((f32[4,64,128]{2,1,0:T(8,128)}), f32[4,64,128]{2,1,0:T(8,128)S(1)}, u32[]{:S(2)}, u32[]{:S(2)}) async-start(f32[4,64,128]{2,1,0:T(8,128)} %bitcast.68), calls=%async_computation.6 | async-start | bytes 262144 | tf_op jit(solution)/shard_map/all_to_all | solution.py:82
  85.3 2.0 %fusion.22 = f32[1,256,1,8,128]{4,1,3,2,0:T(8,128)S(1)} fusion(f32[8,256,128]{2,1,0:T(8,128)} %fusion.74, f32[8,256,128]{2,1,0:T(8,128)} %convolution_add_fusion.1, bf16[8,256,256]{1,2,0:T(8,128)(2,1)S(1)} %fusion.18, bf16[1,256,1,128]{3,1,2,0:T(8,128)(2,1)S(1)} %collective-permute-done.2), kind=kOutput, calls=%fused_computation.32 | convolution fusion | flops 135004160 | bytes 4259840 | tf_op jit(solution)/shard_map/nhgbk,nkhd->nbhgd/dot_general | solution.py:32
  89.8 3.5 %all-to-all-start.5 = ((f32[4,64,1024]{2,1,0:T(8,128)}), f32[4,64,1024]{2,1,0:T(8,128)S(1)}, u32[]{:S(2)}, u32[]{:S(2)}) async-start(f32[4,64,1024]{2,1,0:T(8,128)} %all_to_all.117), calls=%async_computation.5 | async-start | bytes 2097152 | tf_op jit(solution)/shard_map/all_to_all | solution.py:79
  94.7 13.1 %all-to-all-done.5 = f32[4,64,1024]{2,1,0:T(8,128)S(1)} async-done(((f32[4,64,1024]{2,1,0:T(8,128)}), f32[4,64,1024]{2,1,0:T(8,128)S(1)}, u32[]{:S(2)}, u32[]{:S(2)}) %all-to-all-start.5) | async-done | bytes 1048608 | tf_op jit(solution)/shard_map/all_to_all | solution.py:79
  (69 shorter events, 28.7 us)
Async XLA Ops:
  0.6 6.9 %copy-start = (bf16[64,512]{1,0:T(8,128)(2,1)S(1)}, bf16[64,512]{1,0:T(8,128)(2,1)}, u32[]{:S(2)}) copy-start(bf16[64,512]{1,0:T(8,128)(2,1)} %param.7) | copy-start | bytes 196612
  2.0 12.7 %copy-start.4 = (bf16[64,512]{1,0:T(8,128)(2,1)S(1)}, bf16[64,512]{1,0:T(8,128)(2,1)}, u32[]{:S(2)}) copy-start(bf16[64,512]{1,0:T(8,128)(2,1)} %param.8) | copy-start | bytes 196612
  2.0 20.1 %copy-start.3 = (bf16[64,4096]{1,0:T(8,128)(2,1)S(1)}, bf16[64,4096]{1,0:T(8,128)(2,1)}, u32[]{:S(2)}) copy-start(bf16[64,4096]{1,0:T(8,128)(2,1)} %param.6) | copy-start | bytes 1572868
  2.2 27.4 %copy-start.1 = (bf16[64,4096]{1,0:T(8,128)(2,1)S(1)}, bf16[64,4096]{1,0:T(8,128)(2,1)}, u32[]{:S(2)}) copy-start(bf16[64,4096]{1,0:T(8,128)(2,1)} %param.10) | copy-start | bytes 1572868
  3.3 8.1 %all-to-all-start.4 = ((f32[4,1,512]{2,1,0:T(1,128)}), f32[4,1,512]{2,1,0:T(1,128)S(1)}, u32[]{:S(2)}, u32[]{:S(2)}) async-start(f32[4,1,512]{2,1,0:T(1,128)} %reshape.241), calls=%async_computation.4 | async-start | bytes 16384 | tf_op jit(solution)/shard_map/all_to_all | solution.py:56
  11.4 7.4 %all-to-all-start = ((bf16[64,4,128]{2,0,1:T(8,128)(2,1)}), bf16[64,4,128]{2,0,1:T(8,128)(2,1)S(1)}, u32[]{:S(2)}, u32[]{:S(2)}) async-start(bf16[64,4,128]{2,0,1:T(8,128)(2,1)} %copy_bitcast_fusion.5), calls=%async_computation | async-start | bytes 131072 | tf_op jit(solution)/shard_map/all_to_all | solution.py:52
  18.8 7.4 %all-to-all-start.2 = ((bf16[64,4,128]{2,0,1:T(8,128)(2,1)}), bf16[64,4,128]{2,0,1:T(8,128)(2,1)S(1)}, u32[]{:S(2)}, u32[]{:S(2)}) async-start(bf16[64,4,128]{2,0,1:T(8,128)(2,1)} %copy_bitcast_fusion.4), calls=%async_computation.2 | async-start | bytes 131072 | tf_op jit(solution)/shard_map/all_to_all | solution.py:53
  26.1 12.3 %all-to-all-start.1 = ((bf16[64,4,1024]{2,0,1:T(8,128)(2,1)}), bf16[64,4,1024]{2,0,1:T(8,128)(2,1)S(1)}, u32[]{:S(2)}, u32[]{:S(2)}) async-start(bf16[64,4,1024]{2,0,1:T(8,128)(2,1)} %bitcast.347), calls=%async_computation.1 | async-start | bytes 1048576 | tf_op jit(solution)/shard_map/all_to_all | solution.py:51
  38.4 12.3 %all-to-all-start.3 = ((bf16[64,4,1024]{2,0,1:T(8,128)(2,1)}), bf16[64,4,1024]{2,0,1:T(8,128)(2,1)S(1)}, u32[]{:S(2)}, u32[]{:S(2)}) async-start(bf16[64,4,1024]{2,0,1:T(8,128)(2,1)} %bitcast.346), calls=%async_computation.3 | async-start | bytes 1048576 | tf_op jit(solution)/shard_map/all_to_all | solution.py:54
  43.1 7.6 %collective-permute-start = (bf16[1,256,1,128]{3,1,2,0:T(8,128)(2,1)S(1)}, bf16[1,256,1,128]{3,1,2,0:T(8,128)(2,1)S(1)}, u32[]{:S(2)}, u32[]{:S(2)}) collective-permute-start(bf16[1,256,1,128]{3,1,2,0:T(8,128)(2,1)S(1)} %bitcast.370), channel_id=1, source_target_pairs={{0,4},{4,0},{8,12},{12,8},{16,20},{20,16},{24,28},{28,24},{1,5},{5... | collective-permute-start | bytes 196616 | tf_op jit(solution)/shard_map/ppermute | solution.py:13
  45.2 19.9 %collective-permute-start.5 = (bf16[1,256,1,128]{3,1,2,0:T(8,128)(2,1)S(1)}, bf16[1,256,1,128]{3,1,2,0:T(8,128)(2,1)S(1)}, u32[]{:S(2)}, u32[]{:S(2)}) collective-permute-start(bf16[1,256,1,128]{3,1,2,0:T(8,128)(2,1)S(1)} %bitcast.376), channel_id=1, source_target_pairs={{0,16},{4,20},{8,24},{12,28},{16,0},{20,4},{24,8},{28,12},{1,17},{... | collective-permute-start | bytes 196616 | tf_op jit(solution)/shard_map/ppermute | solution.py:13
  47.8 9.2 %collective-permute-start.3 = (bf16[1,256,1,128]{3,1,2,0:T(8,128)(2,1)S(1)}, bf16[1,256,1,128]{3,1,2,0:T(8,128)(2,1)S(1)}, u32[]{:S(2)}, u32[]{:S(2)}) collective-permute-start(bf16[1,256,1,128]{3,1,2,0:T(8,128)(2,1)S(1)} %bitcast.377), channel_id=1, source_target_pairs={{0,8},{4,12},{8,0},{12,4},{16,24},{20,28},{24,16},{28,20},{1,9},{5... | collective-permute-start | bytes 196616 | tf_op jit(solution)/shard_map/ppermute | solution.py:13
  49.4 4.5 %collective-permute-start.1 = (bf16[1,256,1,128]{3,1,2,0:T(8,128)(2,1)S(1)}, bf16[1,256,1,128]{3,1,2,0:T(8,128)(2,1)S(1)}, u32[]{:S(2)}, u32[]{:S(2)}) collective-permute-start(bf16[1,256,1,128]{3,1,2,0:T(8,128)(2,1)S(1)} %bitcast.378), channel_id=1, source_target_pairs={{0,4},{4,0},{8,12},{12,8},{16,20},{20,16},{24,28},{28,24},{1,5},{5... | collective-permute-start | bytes 196616 | tf_op jit(solution)/shard_map/ppermute | solution.py:13
  49.9 13.1 %collective-permute-start.4 = (bf16[1,256,1,128]{3,1,2,0:T(8,128)(2,1)S(1)}, bf16[1,256,1,128]{3,1,2,0:T(8,128)(2,1)S(1)}, u32[]{:S(2)}, u32[]{:S(2)}) collective-permute-start(bf16[1,256,1,128]{3,1,2,0:T(8,128)(2,1)S(1)} %bitcast.371), channel_id=1, source_target_pairs={{0,16},{4,20},{8,24},{12,28},{16,0},{20,4},{24,8},{28,12},{1,17},{... | collective-permute-start | bytes 196616 | tf_op jit(solution)/shard_map/ppermute | solution.py:13
  50.8 5.8 %collective-permute-start.2 = (bf16[1,256,1,128]{3,1,2,0:T(8,128)(2,1)S(1)}, bf16[1,256,1,128]{3,1,2,0:T(8,128)(2,1)S(1)}, u32[]{:S(2)}, u32[]{:S(2)}) collective-permute-start(bf16[1,256,1,128]{3,1,2,0:T(8,128)(2,1)S(1)} %bitcast.372), channel_id=1, source_target_pairs={{0,8},{4,12},{8,0},{12,4},{16,24},{20,28},{24,16},{28,20},{1,9},{5... | collective-permute-start | bytes 196616 | tf_op jit(solution)/shard_map/ppermute | solution.py:13
  55.0 22.4 %collective-permute-start.6 = (f32[1,256,1,128]{3,1,2,0:T(8,128)S(1)}, f32[1,256,1,128]{3,1,2,0:T(8,128)S(1)}, u32[]{:S(2)}, u32[]{:S(2)}) collective-permute-start(f32[1,256,1,128]{3,1,2,0:T(8,128)S(1)} %fusion.28), channel_id=1, source_target_pairs={{0,4},{4,0},{8,12},{12,8},{16,20},{20,16},{24,28},{28,24},{1,5},{5... | collective-permute-start | bytes 393224 | tf_op jit(solution)/shard_map/ppermute | solution.py:13
  58.7 18.7 %collective-permute-start.7 = (f32[1,256,1,128]{3,1,2,0:T(8,128)}, f32[1,256,1,128]{3,1,2,0:T(8,128)S(1)}, u32[]{:S(2)}, u32[]{:S(2)}) collective-permute-start(f32[1,256,1,128]{3,1,2,0:T(8,128)} %fusion.26), channel_id=1, source_target_pairs={{0,8},{4,12},{8,0},{12,4},{16,24},{20,28},{24,16},{28,20},{1,9},{5... | collective-permute-start | bytes 393224 | tf_op jit(solution)/shard_map/ppermute | solution.py:13
  61.4 10.4 %collective-permute-start.9 = (f32[1,256,1,128]{3,1,2,0:T(8,128)S(1)}, f32[1,256,1,128]{3,1,2,0:T(8,128)S(1)}, u32[]{:S(2)}, u32[]{:S(2)}) collective-permute-start(f32[1,256,1,128]{3,1,2,0:T(8,128)S(1)} %convolution_bitcast_fusion.2), channel_id=1, source_target_pairs={{0,4},{4,0},{8,12},{12,8},{16,20},{20,16},{24,28},{28,24},{1,5},{5... | collective-permute-start | bytes 393224 | tf_op jit(solution)/shard_map/ppermute | solution.py:13
  63.0 9.8 %collective-permute-start.10 = (f32[1,256,1,128]{3,1,2,0:T(8,128)S(1)}, f32[1,256,1,128]{3,1,2,0:T(8,128)S(1)}, u32[]{:S(2)}, u32[]{:S(2)}) collective-permute-start(f32[1,256,1,128]{3,1,2,0:T(8,128)S(1)} %convolution_bitcast_fusion.1), channel_id=1, source_target_pairs={{0,8},{4,12},{8,0},{12,4},{16,24},{20,28},{24,16},{28,20},{1,9},{5... | collective-permute-start | bytes 393224 | tf_op jit(solution)/shard_map/ppermute | solution.py:13
  65.1 7.7 %collective-permute-start.11 = (f32[1,256,1,128]{3,1,2,0:T(8,128)S(1)}, f32[1,256,1,128]{3,1,2,0:T(8,128)S(1)}, u32[]{:S(2)}, u32[]{:S(2)}) collective-permute-start(f32[1,256,1,128]{3,1,2,0:T(8,128)S(1)} %convolution_bitcast_fusion), channel_id=1, source_target_pairs={{0,16},{4,20},{8,24},{12,28},{16,0},{20,4},{24,8},{28,12},{1,17},{... | collective-permute-start | bytes 393224 | tf_op jit(solution)/shard_map/ppermute | solution.py:13
  71.8 7.5 %collective-permute-start.8 = (f32[1,256,1,128]{3,1,2,0:T(8,128)}, f32[1,256,1,128]{3,1,2,0:T(8,128)S(1)}, u32[]{:S(2)}, u32[]{:S(2)}) collective-permute-start(f32[1,256,1,128]{3,1,2,0:T(8,128)} %fusion.24), channel_id=1, source_target_pairs={{0,16},{4,20},{8,24},{12,28},{16,0},{20,4},{24,8},{28,12},{1,17},{... | collective-permute-start | bytes 393224 | tf_op jit(solution)/shard_map/ppermute | solution.py:13
  74.0 7.9 %all-to-all-start.7 = ((f32[4,64,128]{2,1,0:T(8,128)}), f32[4,64,128]{2,1,0:T(8,128)S(1)}, u32[]{:S(2)}, u32[]{:S(2)}) async-start(f32[4,64,128]{2,1,0:T(8,128)} %bitcast.90), calls=%async_computation.7 | async-start | bytes 262144 | tf_op jit(solution)/shard_map/all_to_all | solution.py:85
  81.9 7.9 %all-to-all-start.6 = ((f32[4,64,128]{2,1,0:T(8,128)}), f32[4,64,128]{2,1,0:T(8,128)S(1)}, u32[]{:S(2)}, u32[]{:S(2)}) async-start(f32[4,64,128]{2,1,0:T(8,128)} %bitcast.68), calls=%async_computation.6 | async-start | bytes 262144 | tf_op jit(solution)/shard_map/all_to_all | solution.py:82
  89.8 17.9 %all-to-all-start.5 = ((f32[4,64,1024]{2,1,0:T(8,128)}), f32[4,64,1024]{2,1,0:T(8,128)S(1)}, u32[]{:S(2)}, u32[]{:S(2)}) async-start(f32[4,64,1024]{2,1,0:T(8,128)} %all_to_all.117), calls=%async_computation.5 | async-start | bytes 2097152 | tf_op jit(solution)/shard_map/all_to_all | solution.py:79
  (1 other events, 3.0 us)
where the time goes:
time: 110 us; the launch traced here: 109 us
  starting transfers between devices  44.9 us (41%)
  waiting for transfers between devices  35.4 us (32%)
  matrix products  16.3 us (15%)
  local copies, waits for them, and re-layouts  8.94 us (8%)
  other arithmetic  2.35 us (2%)
    ppermute x12, starting transfers between devices, from_partner(): lax.ppermute(value, axis, [(i, i ^ 1 << distance) for i in range(lax.axis...  17 us
    all_to_all x1, waiting for transfers between devices, on_device(): lax.all_to_all(grad_q.reshape(row_count, -1), 'head', split_axis=0, conca...  13.1 us
    all_to_all x1, waiting for transfers between devices, on_device(): lax.all_to_all(queries, 'head', split_axis=1, concat_axis=0, tiled=True)  7.92 us
    dot_general x4, matrix products, block_grads(): jnp.einsum('nhgbk,nkhd->nbhgd', dscores, key_blk, preferred_element_type=...  5.48 us
    all_to_all x1, starting transfers between devices, on_device(): lax.all_to_all(dot_before, 'head', split_axis=1, concat_axis=0, tiled=True)  4.24 us
    dot_general x4, matrix products, block_grads(): jnp.einsum('nhgbk,nbhgd->nkhd', dscores, query_blk, preferred_element_typ...  3.69 us
    all_to_all x1, starting transfers between devices, on_device(): lax.all_to_all(grad_q.reshape(row_count, -1), 'head', split_axis=0, conca...  3.52 us
    all_to_all x1, starting transfers between devices, on_device(): lax.all_to_all(queries, 'head', split_axis=1, concat_axis=0, tiled=True)  3.47 us
  transfers between devices with their start and end apart: 20, of which 9 were waited for; matrix products, arithmetic and copies ran while one was open for 21% of the time, Pallas kernels for 0%

commit v1 on v0

--- a/solution.py
+++ b/solution.py
@@ -7,6 +7,28 @@
 HEAD_DIM = 128
 GROUP = 8
 BLOCK = 256
+
+
+def in_blocks(array, dim, devices):
+    before, after = (array.shape[:dim], array.shape[dim + 1 :])
+    return jnp.moveaxis(array.reshape(*before, devices, -1, *after), dim, 0)
+
+
+def joined_along(blocks, dim):
+    shape = list(blocks.shape[1:])
+    shape[dim] *= blocks.shape[0]
+    return jnp.moveaxis(blocks, 0, dim).reshape(shape)
+
+
+def pairwise_exchange(shard, axis, split_dim, concat_dim):
+    count, mine = (lax.axis_size(axis), lax.axis_index(axis))
+    pieces = in_blocks(shard, split_dim, count)
+    done = [pieces[mine]]
+    for turn in range(1, count):
+        sent = pieces[mine ^ turn]
+        done.append(lax.ppermute(sent, axis, [(i, i ^ turn) for i in range(count)]))
+    pieces = jnp.stack(done)[mine ^ jnp.arange(count)]
+    return joined_along(pieces, concat_dim)
 
 
 def from_partner(value, axis, distance):
@@ -49,7 +71,7 @@
     )
     q_local, k_local, v_local, g_local = (
         lax.all_to_all(queries, "head", split_axis=1, concat_axis=0, tiled=True),
-        lax.all_to_all(key_rows, "head", split_axis=1, concat_axis=0, tiled=True),
+        pairwise_exchange(key_rows, "head", 1, 0),
         lax.all_to_all(value_rows, "head", split_axis=1, concat_axis=0, tiled=True),
         lax.all_to_all(out_grad, "head", split_axis=1, concat_axis=0, tiled=True),
     )

time: 110 us -> 105 us (0.955)
  the two profiles are of different devices: /device:TPU:0 before, /device:TPU:24 now
where the time goes in v1:
time: 105 us
  starting transfers between devices  41.2 us (39%)
  waiting for transfers between devices  35.7 us (34%)
  matrix products  15.6 us (15%)
  local copies, waits for them, and re-layouts  8.84 us (8%)
  other arithmetic  2.38 us (2%)
    ppermute x12, starting transfers between devices, from_partner(): lax.ppermute(value, axis, [(i, i ^ 1 << distance) for i in range(lax.axis...  15.3 us
    all_to_all x1, waiting for transfers between devices, on_device(): lax.all_to_all(grad_q.reshape(row_count, -1), 'head', split_axis=0, conca...  13.1 us
    all_to_all x1, waiting for transfers between devices, on_device(): lax.all_to_all(queries, 'head', split_axis=1, concat_axis=0, tiled=True)  5.81 us
    ppermute x12, waiting for transfers between devices, from_partner(): lax.ppermute(value, axis, [(i, i ^ 1 << distance) for i in range(lax.axis...  5.76 us
    dot_general x4, matrix products, block_grads(): jnp.einsum('nhgbk,nkhd->nbhgd', dscores, key_blk, preferred_element_type=...  4.84 us
    dot_general x4, matrix products, block_grads(): jnp.einsum('nhgbk,nbhgd->nkhd', dscores, query_blk, preferred_element_typ...  3.7 us
    all_to_all x1, starting transfers between devices, on_device(): lax.all_to_all(grad_q.reshape(row_count, -1), 'head', split_axis=0, conca...  3.52 us
    all_to_all x1, starting transfers between devices, on_device(): lax.all_to_all(queries, 'head', split_axis=1, concat_axis=0, tiled=True)  3.47 us
  transfers between devices with their start and end apart: 22, of which 9 were waited for; matrix products, arithmetic and copies ran while one was open for 21% of the time, Pallas kernels for 0%

profile of v1, /device:TPU:24, one launch (start us, length us, event | category | flops | bytes accessed | tf_op | source)
XLA Modules:
  0.0 104.8 jit_solution(14926386399862688204)
XLA Ops:
  0.6 1.3 %multiply_bitcast_fusion = f32[8,8,32,128]{3,1,2,0:T(8,128)S(1)} fusion(bf16[64,4096]{1,0:T(8,128)(2,1)} %param.9, bf16[64,4096]{1,0:T(8,128)(2,1)} %param.10), kind=kLoop, calls=%fused_computation.60 | loop fusion | flops 786432 | bytes 2097152
  3.3 3.2 %all-to-all-start.3 = ((f32[4,1,512]{2,1,0:T(1,128)}), f32[4,1,512]{2,1,0:T(1,128)S(1)}, u32[]{:S(2)}, u32[]{:S(2)}) async-start(f32[4,1,512]{2,1,0:T(1,128)} %reshape.272), calls=%async_computation.3 | async-start | bytes 16384 | tf_op jit(solution)/shard_map/all_to_all | solution.py:78
  7.2 3.1 %all-to-all-done.3 = f32[4,1,512]{2,1,0:T(1,128)S(1)} async-done(((f32[4,1,512]{2,1,0:T(1,128)}), f32[4,1,512]{2,1,0:T(1,128)S(1)}, u32[]{:S(2)}, u32[]{:S(2)}) %all-to-all-start.3) | async-done | bytes 8224 | tf_op jit(solution)/shard_map/all_to_all | solution.py:78
  10.4 3.3 %all-to-all-start.1 = ((bf16[64,4,128]{2,0,1:T(8,128)(2,1)}), bf16[64,4,128]{2,0,1:T(8,128)(2,1)S(1)}, u32[]{:S(2)}, u32[]{:S(2)}) async-start(bf16[64,4,128]{2,0,1:T(8,128)(2,1)} %copy_bitcast_fusion.4), calls=%async_computation.1 | async-start | bytes 131072 | tf_op jit(solution)/shard_map/all_to_all | solution.py:75
  14.5 3.2 %all-to-all-done.1 = bf16[64,4,128]{2,0,1:T(8,128)(2,1)S(1)} async-done(((bf16[64,4,128]{2,0,1:T(8,128)(2,1)}), bf16[64,4,128]{2,0,1:T(8,128)(2,1)S(1)}, u32[]{:S(2)}, u32[]{:S(2)}) %all-to-all-start.1) | async-done | bytes 65568 | tf_op jit(solution)/shard_map/all_to_all | solution.py:75
  17.7 3.5 %all-to-all-start = ((bf16[64,4,1024]{2,0,1:T(8,128)(2,1)}), bf16[64,4,1024]{2,0,1:T(8,128)(2,1)S(1)}, u32[]{:S(2)}, u32[]{:S(2)}) async-start(bf16[64,4,1024]{2,0,1:T(8,128)(2,1)} %bitcast.354), calls=%async_computation | async-start | bytes 1048576 | tf_op jit(solution)/shard_map/all_to_all | solution.py:73
  22.0 1.6 %collective-permute-start.1 = (bf16[64,128]{1,0:T(8,128)(2,1)S(1)}, bf16[64,128]{1,0:T(8,128)(2,1)S(1)}, u32[]{:S(2)}, u32[]{:S(2)}) collective-permute-start(bf16[64,128]{1,0:T(8,128)(2,1)S(1)} %bitcast.397), channel_id=1, source_target_pairs={{0,2},{1,3},{2,0},{3,1},{4,6},{5,7},{6,4},{7,5},{8,10},{9,11},{10,... | collective-permute-start | bytes 49160 | tf_op jit(solution)/shard_map/ppermute | solution.py:29
  24.5 5.8 %all-to-all-done = bf16[64,4,1024]{2,0,1:T(8,128)(2,1)S(1)} async-done(((bf16[64,4,1024]{2,0,1:T(8,128)(2,1)}), bf16[64,4,1024]{2,0,1:T(8,128)(2,1)S(1)}, u32[]{:S(2)}, u32[]{:S(2)}) %all-to-all-start) | async-done | bytes 524320 | tf_op jit(solution)/shard_map/all_to_all | solution.py:73
  30.4 3.5 %all-to-all-start.2 = ((bf16[64,4,1024]{2,0,1:T(8,128)(2,1)}), bf16[64,4,1024]{2,0,1:T(8,128)(2,1)S(1)}, u32[]{:S(2)}, u32[]{:S(2)}) async-start(bf16[64,4,1024]{2,0,1:T(8,128)(2,1)} %bitcast.353), calls=%async_computation.2 | async-start | bytes 1048576 | tf_op jit(solution)/shard_map/all_to_all | solution.py:76
  35.7 1.6 %collective-permute-start.3 = (bf16[1,256,1,128]{3,1,2,0:T(8,128)(2,1)S(1)}, bf16[1,256,1,128]{3,1,2,0:T(8,128)(2,1)S(1)}, u32[]{:S(2)}, u32[]{:S(2)}) collective-permute-start(bf16[1,256,1,128]{3,1,2,0:T(8,128)(2,1)S(1)} %bitcast.381), channel_id=1, source_target_pairs={{0,4},{4,0},{8,12},{12,8},{16,20},{20,16},{24,28},{28,24},{1,5},{5... | collective-permute-start | bytes 196616 | tf_op jit(solution)/shard_map/ppermute | solution.py:35
  38.2 2.6 %collective-permute-start.8 = (bf16[1,256,1,128]{3,1,2,0:T(8,128)(2,1)S(1)}, bf16[1,256,1,128]{3,1,2,0:T(8,128)(2,1)S(1)}, u32[]{:S(2)}, u32[]{:S(2)}) collective-permute-start(bf16[1,256,1,128]{3,1,2,0:T(8,128)(2,1)S(1)} %bitcast.387), channel_id=1, source_target_pairs={{0,16},{4,20},{8,24},{12,28},{16,0},{20,4},{24,8},{28,12},{1,17},{... | collective-permute-start | bytes 196616 | tf_op jit(solution)/shard_map/ppermute | solution.py:35
  40.8 1.6 %collective-permute-start.6 = (bf16[1,256,1,128]{3,1,2,0:T(8,128)(2,1)S(1)}, bf16[1,256,1,128]{3,1,2,0:T(8,128)(2,1)S(1)}, u32[]{:S(2)}, u32[]{:S(2)}) collective-permute-start(bf16[1,256,1,128]{3,1,2,0:T(8,128)(2,1)S(1)} %bitcast.388), channel_id=1, source_target_pairs={{0,8},{4,12},{8,0},{12,4},{16,24},{20,28},{24,16},{28,20},{1,9},{5... | collective-permute-start | bytes 196616 | tf_op jit(solution)/shard_map/ppermute | solution.py:35
  42.7 1.6 %collective-permute-start.4 = (bf16[1,256,1,128]{3,1,2,0:T(8,128)(2,1)S(1)}, bf16[1,256,1,128]{3,1,2,0:T(8,128)(2,1)S(1)}, u32[]{:S(2)}, u32[]{:S(2)}) collective-permute-start(bf16[1,256,1,128]{3,1,2,0:T(8,128)(2,1)S(1)} %bitcast.389), channel_id=1, source_target_pairs={{0,4},{4,0},{8,12},{12,8},{16,20},{20,16},{24,28},{28,24},{1,5},{5... | collective-permute-start | bytes 196616 | tf_op jit(solution)/shard_map/ppermute | solution.py:35
  45.3 1.7 %collective-permute-done.4 = bf16[1,256,1,128]{3,1,2,0:T(8,128)(2,1)S(1)} collective-permute-done((bf16[1,256,1,128]{3,1,2,0:T(8,128)(2,1)S(1)}, bf16[1,256,1,128]{3,1,2,0:T(8,128)(2,1)S(1)}, u32[]{:S(2)}, u32[]{:S(2)}) %collective-permute-start.4) | collective-permute-done | bytes 65568 | tf_op jit(solution)/shard_map/ppermute | solution.py:35
  48.1 1.6 %collective-permute-start.9 = (f32[1,256,1,128]{3,1,2,0:T(8,128)S(1)}, f32[1,256,1,128]{3,1,2,0:T(8,128)S(1)}, u32[]{:S(2)}, u32[]{:S(2)}) collective-permute-start(f32[1,256,1,128]{3,1,2,0:T(8,128)S(1)} %fusion.28), channel_id=1, source_target_pairs={{0,4},{4,0},{8,12},{12,8},{16,20},{20,16},{24,28},{28,24},{1,5},{5... | collective-permute-start | bytes 393224 | tf_op jit(solution)/shard_map/ppermute | solution.py:35
  54.9 1.6 %collective-permute-start.13 = (f32[1,256,1,128]{3,1,2,0:T(8,128)S(1)}, f32[1,256,1,128]{3,1,2,0:T(8,128)S(1)}, u32[]{:S(2)}, u32[]{:S(2)}) collective-permute-start(f32[1,256,1,128]{3,1,2,0:T(8,128)S(1)} %convolution_bitcast_fusion.1), channel_id=1, source_target_pairs={{0,8},{4,12},{8,0},{12,4},{16,24},{20,28},{24,16},{28,20},{1,9},{5... | collective-permute-start | bytes 393224 | tf_op jit(solution)/shard_map/ppermute | solution.py:35
  62.2 2.6 %collective-permute-start.11 = (f32[1,256,1,128]{3,1,2,0:T(8,128)}, f32[1,256,1,128]{3,1,2,0:T(8,128)S(1)}, u32[]{:S(2)}, u32[]{:S(2)}) collective-permute-start(f32[1,256,1,128]{3,1,2,0:T(8,128)} %fusion.24), channel_id=1, source_target_pairs={{0,16},{4,20},{8,24},{12,28},{16,0},{20,4},{24,8},{28,12},{1,17},{... | collective-permute-start | bytes 393224 | tf_op jit(solution)/shard_map/ppermute | solution.py:35
  64.8 4.0 %collective-permute-done.14 = f32[1,256,1,128]{3,1,2,0:T(8,128)S(1)} collective-permute-done((f32[1,256,1,128]{3,1,2,0:T(8,128)S(1)}, f32[1,256,1,128]{3,1,2,0:T(8,128)S(1)}, u32[]{:S(2)}, u32[]{:S(2)}) %collective-permute-start.14) | collective-permute-done | bytes 131104 | tf_op jit(solution)/shard_map/ppermute | solution.py:35
  70.0 3.3 %all-to-all-start.6 = ((f32[4,64,128]{2,1,0:T(8,128)}), f32[4,64,128]{2,1,0:T(8,128)S(1)}, u32[]{:S(2)}, u32[]{:S(2)}) async-start(f32[4,64,128]{2,1,0:T(8,128)} %bitcast.95), calls=%async_computation.6 | async-start | bytes 262144 | tf_op jit(solution)/shard_map/all_to_all | solution.py:107
  74.5 3.4 %all-to-all-done.6 = f32[4,64,128]{2,1,0:T(8,128)S(1)} async-done(((f32[4,64,128]{2,1,0:T(8,128)}), f32[4,64,128]{2,1,0:T(8,128)S(1)}, u32[]{:S(2)}, u32[]{:S(2)}) %all-to-all-start.6) | async-done | bytes 131104 | tf_op jit(solution)/shard_map/all_to_all | solution.py:107
  77.9 3.3 %all-to-all-start.5 = ((f32[4,64,128]{2,1,0:T(8,128)}), f32[4,64,128]{2,1,0:T(8,128)S(1)}, u32[]{:S(2)}, u32[]{:S(2)}) async-start(f32[4,64,128]{2,1,0:T(8,128)} %bitcast.73), calls=%async_computation.5 | async-start | bytes 262144 | tf_op jit(solution)/shard_map/all_to_all | solution.py:104
  81.2 1.9 %fusion.22 = f32[1,256,1,8,128]{1,4,3,2,0:T(8,128)S(1)} fusion(f32[128,8,256]{2,0,1:T(8,128)} %fusion.75, f32[128,8,256]{2,0,1:T(8,128)} %convolution_add_fusion.1, bf16[8,256,256]{1,2,0:T(8,128)(2,1)S(1)} %fusion.18, bf16[1,256,1,128]{3,1,2,0:T(8,128)(2,1)S(1)} %collective-permute-done.5), kind=kOutput, calls=%fused_computation.33 | convolution fusion | flops 135004160 | bytes 4259840 | tf_op jit(solution)/shard_map/nhgbk,nkhd->nbhgd/dot_general | solution.py:54
  85.8 3.5 %all-to-all-start.4 = ((f32[4,64,1024]{2,1,0:T(8,128)}), f32[4,64,1024]{2,1,0:T(8,128)S(1)}, u32[]{:S(2)}, u32[]{:S(2)}) async-start(f32[4,64,1024]{2,1,0:T(8,128)} %all_to_all.102), calls=%async_computation.4 | async-start | bytes 2097152 | tf_op jit(solution)/shard_map/all_to_all | solution.py:101
  90.7 13.1 %all-to-all-done.4 = f32[4,64,1024]{2,1,0:T(8,128)S(1)} async-done(((f32[4,64,1024]{2,1,0:T(8,128)}), f32[4,64,1024]{2,1,0:T(8,128)S(1)}, u32[]{:S(2)}, u32[]{:S(2)}) %all-to-all-start.4) | async-done | bytes 1048608 | tf_op jit(solution)/shard_map/all_to_all | solution.py:101
  (82 shorter events, 27.7 us)
Async XLA Ops:
  2.2 19.1 %copy-start.4 = (bf16[64,512]{1,0:T(8,128)(2,1)S(1)}, bf16[64,512]{1,0:T(8,128)(2,1)}, u32[]{:S(2)}) copy-start(bf16[64,512]{1,0:T(8,128)(2,1)} %param.7) | copy-start | bytes 196612
  2.2 21.5 %copy-start.1 = (bf16[64,4096]{1,0:T(8,128)(2,1)S(1)}, bf16[64,4096]{1,0:T(8,128)(2,1)}, u32[]{:S(2)}) copy-start(bf16[64,4096]{1,0:T(8,128)(2,1)} %param.10) | copy-start | bytes 1572868
  3.3 7.0 %all-to-all-start.3 = ((f32[4,1,512]{2,1,0:T(1,128)}), f32[4,1,512]{2,1,0:T(1,128)S(1)}, u32[]{:S(2)}, u32[]{:S(2)}) async-start(f32[4,1,512]{2,1,0:T(1,128)} %reshape.272), calls=%async_computation.3 | async-start | bytes 16384 | tf_op jit(solution)/shard_map/all_to_all | solution.py:78
  10.4 7.4 %all-to-all-start.1 = ((bf16[64,4,128]{2,0,1:T(8,128)(2,1)}), bf16[64,4,128]{2,0,1:T(8,128)(2,1)S(1)}, u32[]{:S(2)}, u32[]{:S(2)}) async-start(bf16[64,4,128]{2,0,1:T(8,128)(2,1)} %copy_bitcast_fusion.4), calls=%async_computation.1 | async-start | bytes 131072 | tf_op jit(solution)/shard_map/all_to_all | solution.py:75
  17.7 12.6 %all-to-all-start = ((bf16[64,4,1024]{2,0,1:T(8,128)(2,1)}), bf16[64,4,1024]{2,0,1:T(8,128)(2,1)S(1)}, u32[]{:S(2)}, u32[]{:S(2)}) async-start(bf16[64,4,1024]{2,0,1:T(8,128)(2,1)} %bitcast.354), calls=%async_computation | async-start | bytes 1048576 | tf_op jit(solution)/shard_map/all_to_all | solution.py:73
  21.5 13.7 %collective-permute-start = (bf16[64,128]{1,0:T(8,128)(2,1)S(1)}, bf16[64,128]{1,0:T(8,128)(2,1)S(1)}, u32[]{:S(2)}, u32[]{:S(2)}) collective-permute-start(bf16[64,128]{1,0:T(8,128)(2,1)S(1)} %bitcast.396), channel_id=1, source_target_pairs={{0,1},{1,0},{2,3},{3,2},{4,5},{5,4},{6,7},{7,6},{8,9},{9,8},{10,11... | collective-permute-start | bytes 49160 | tf_op jit(solution)/shard_map/ppermute | solution.py:29
  22.0 13.2 %collective-permute-start.1 = (bf16[64,128]{1,0:T(8,128)(2,1)S(1)}, bf16[64,128]{1,0:T(8,128)(2,1)S(1)}, u32[]{:S(2)}, u32[]{:S(2)}) collective-permute-start(bf16[64,128]{1,0:T(8,128)(2,1)S(1)} %bitcast.397), channel_id=1, source_target_pairs={{0,2},{1,3},{2,0},{3,1},{4,6},{5,7},{6,4},{7,5},{8,10},{9,11},{10,... | collective-permute-start | bytes 49160 | tf_op jit(solution)/shard_map/ppermute | solution.py:29
  23.6 11.5 %collective-permute-start.2 = (bf16[64,128]{1,0:T(8,128)(2,1)S(1)}, bf16[64,128]{1,0:T(8,128)(2,1)S(1)}, u32[]{:S(2)}, u32[]{:S(2)}) collective-permute-start(bf16[64,128]{1,0:T(8,128)(2,1)S(1)} %bitcast.398), channel_id=1, source_target_pairs={{0,3},{1,2},{2,1},{3,0},{4,7},{5,6},{6,5},{7,4},{8,11},{9,10},{10,... | collective-permute-start | bytes 49160 | tf_op jit(solution)/shard_map/ppermute | solution.py:29
  30.4 12.3 %all-to-all-start.2 = ((bf16[64,4,1024]{2,0,1:T(8,128)(2,1)}), bf16[64,4,1024]{2,0,1:T(8,128)(2,1)S(1)}, u32[]{:S(2)}, u32[]{:S(2)}) async-start(bf16[64,4,1024]{2,0,1:T(8,128)(2,1)} %bitcast.353), calls=%async_computation.2 | async-start | bytes 1048576 | tf_op jit(solution)/shard_map/all_to_all | solution.py:76
  35.7 7.0 %collective-permute-start.3 = (bf16[1,256,1,128]{3,1,2,0:T(8,128)(2,1)S(1)}, bf16[1,256,1,128]{3,1,2,0:T(8,128)(2,1)S(1)}, u32[]{:S(2)}, u32[]{:S(2)}) collective-permute-start(bf16[1,256,1,128]{3,1,2,0:T(8,128)(2,1)S(1)} %bitcast.381), channel_id=1, source_target_pairs={{0,4},{4,0},{8,12},{12,8},{16,20},{20,16},{24,28},{28,24},{1,5},{5... | collective-permute-start | bytes 196616 | tf_op jit(solution)/shard_map/ppermute | solution.py:35
  37.4 17.4 %collective-permute-start.7 = (bf16[1,256,1,128]{3,1,2,0:T(8,128)(2,1)S(1)}, bf16[1,256,1,128]{3,1,2,0:T(8,128)(2,1)S(1)}, u32[]{:S(2)}, u32[]{:S(2)}) collective-permute-start(bf16[1,256,1,128]{3,1,2,0:T(8,128)(2,1)S(1)} %bitcast.382), channel_id=1, source_target_pairs={{0,16},{4,20},{8,24},{12,28},{16,0},{20,4},{24,8},{28,12},{1,17},{... | collective-permute-start | bytes 196616 | tf_op jit(solution)/shard_map/ppermute | solution.py:35
  37.8 11.9 %collective-permute-start.5 = (bf16[1,256,1,128]{3,1,2,0:T(8,128)(2,1)S(1)}, bf16[1,256,1,128]{3,1,2,0:T(8,128)(2,1)S(1)}, u32[]{:S(2)}, u32[]{:S(2)}) collective-permute-start(bf16[1,256,1,128]{3,1,2,0:T(8,128)(2,1)S(1)} %bitcast.383), channel_id=1, source_target_pairs={{0,8},{4,12},{8,0},{12,4},{16,24},{20,28},{24,16},{28,20},{1,9},{5... | collective-permute-start | bytes 196616 | tf_op jit(solution)/shard_map/ppermute | solution.py:35
  38.2 19.2 %collective-permute-start.8 = (bf16[1,256,1,128]{3,1,2,0:T(8,128)(2,1)S(1)}, bf16[1,256,1,128]{3,1,2,0:T(8,128)(2,1)S(1)}, u32[]{:S(2)}, u32[]{:S(2)}) collective-permute-start(bf16[1,256,1,128]{3,1,2,0:T(8,128)(2,1)S(1)} %bitcast.387), channel_id=1, source_target_pairs={{0,16},{4,20},{8,24},{12,28},{16,0},{20,4},{24,8},{28,12},{1,17},{... | collective-permute-start | bytes 196616 | tf_op jit(solution)/shard_map/ppermute | solution.py:35
  40.8 9.4 %collective-permute-start.6 = (bf16[1,256,1,128]{3,1,2,0:T(8,128)(2,1)S(1)}, bf16[1,256,1,128]{3,1,2,0:T(8,128)(2,1)S(1)}, u32[]{:S(2)}, u32[]{:S(2)}) collective-permute-start(bf16[1,256,1,128]{3,1,2,0:T(8,128)(2,1)S(1)} %bitcast.388), channel_id=1, source_target_pairs={{0,8},{4,12},{8,0},{12,4},{16,24},{20,28},{24,16},{28,20},{1,9},{5... | collective-permute-start | bytes 196616 | tf_op jit(solution)/shard_map/ppermute | solution.py:35
  42.7 4.3 %collective-permute-start.4 = (bf16[1,256,1,128]{3,1,2,0:T(8,128)(2,1)S(1)}, bf16[1,256,1,128]{3,1,2,0:T(8,128)(2,1)S(1)}, u32[]{:S(2)}, u32[]{:S(2)}) collective-permute-start(bf16[1,256,1,128]{3,1,2,0:T(8,128)(2,1)S(1)} %bitcast.389), channel_id=1, source_target_pairs={{0,4},{4,0},{8,12},{12,8},{16,20},{20,16},{24,28},{28,24},{1,5},{5... | collective-permute-start | bytes 196616 | tf_op jit(solution)/shard_map/ppermute | solution.py:35
  48.1 25.2 %collective-permute-start.9 = (f32[1,256,1,128]{3,1,2,0:T(8,128)S(1)}, f32[1,256,1,128]{3,1,2,0:T(8,128)S(1)}, u32[]{:S(2)}, u32[]{:S(2)}) collective-permute-start(f32[1,256,1,128]{3,1,2,0:T(8,128)S(1)} %fusion.28), channel_id=1, source_target_pairs={{0,4},{4,0},{8,12},{12,8},{16,20},{20,16},{24,28},{28,24},{1,5},{5... | collective-permute-start | bytes 393224 | tf_op jit(solution)/shard_map/ppermute | solution.py:35
  51.9 21.5 %collective-permute-start.10 = (f32[1,256,1,128]{3,1,2,0:T(8,128)}, f32[1,256,1,128]{3,1,2,0:T(8,128)S(1)}, u32[]{:S(2)}, u32[]{:S(2)}) collective-permute-start(f32[1,256,1,128]{3,1,2,0:T(8,128)} %fusion.26), channel_id=1, source_target_pairs={{0,8},{4,12},{8,0},{12,4},{16,24},{20,28},{24,16},{28,20},{1,9},{5... | collective-permute-start | bytes 393224 | tf_op jit(solution)/shard_map/ppermute | solution.py:35
  54.3 7.9 %collective-permute-start.12 = (f32[1,256,1,128]{3,1,2,0:T(8,128)S(1)}, f32[1,256,1,128]{3,1,2,0:T(8,128)S(1)}, u32[]{:S(2)}, u32[]{:S(2)}) collective-permute-start(f32[1,256,1,128]{3,1,2,0:T(8,128)S(1)} %convolution_bitcast_fusion.2), channel_id=1, source_target_pairs={{0,4},{4,0},{8,12},{12,8},{16,20},{20,16},{24,28},{28,24},{1,5},{5... | collective-permute-start | bytes 393224 | tf_op jit(solution)/shard_map/ppermute | solution.py:35
  54.9 9.9 %collective-permute-start.13 = (f32[1,256,1,128]{3,1,2,0:T(8,128)S(1)}, f32[1,256,1,128]{3,1,2,0:T(8,128)S(1)}, u32[]{:S(2)}, u32[]{:S(2)}) collective-permute-start(f32[1,256,1,128]{3,1,2,0:T(8,128)S(1)} %convolution_bitcast_fusion.1), channel_id=1, source_target_pairs={{0,8},{4,12},{8,0},{12,4},{16,24},{20,28},{24,16},{28,20},{1,9},{5... | collective-permute-start | bytes 393224 | tf_op jit(solution)/shard_map/ppermute | solution.py:35
  57.4 11.3 %collective-permute-start.14 = (f32[1,256,1,128]{3,1,2,0:T(8,128)S(1)}, f32[1,256,1,128]{3,1,2,0:T(8,128)S(1)}, u32[]{:S(2)}, u32[]{:S(2)}) collective-permute-start(f32[1,256,1,128]{3,1,2,0:T(8,128)S(1)} %convolution_bitcast_fusion), channel_id=1, source_target_pairs={{0,16},{4,20},{8,24},{12,28},{16,0},{20,4},{24,8},{28,12},{1,17},{... | collective-permute-start | bytes 393224 | tf_op jit(solution)/shard_map/ppermute | solution.py:35
  62.2 11.2 %collective-permute-start.11 = (f32[1,256,1,128]{3,1,2,0:T(8,128)}, f32[1,256,1,128]{3,1,2,0:T(8,128)S(1)}, u32[]{:S(2)}, u32[]{:S(2)}) collective-permute-start(f32[1,256,1,128]{3,1,2,0:T(8,128)} %fusion.24), channel_id=1, source_target_pairs={{0,16},{4,20},{8,24},{12,28},{16,0},{20,4},{24,8},{28,12},{1,17},{... | collective-permute-start | bytes 393224 | tf_op jit(solution)/shard_map/ppermute | solution.py:35
  70.0 7.9 %all-to-all-start.6 = ((f32[4,64,128]{2,1,0:T(8,128)}), f32[4,64,128]{2,1,0:T(8,128)S(1)}, u32[]{:S(2)}, u32[]{:S(2)}) async-start(f32[4,64,128]{2,1,0:T(8,128)} %bitcast.95), calls=%async_computation.6 | async-start | bytes 262144 | tf_op jit(solution)/shard_map/all_to_all | solution.py:107
  77.9 7.9 %all-to-all-start.5 = ((f32[4,64,128]{2,1,0:T(8,128)}), f32[4,64,128]{2,1,0:T(8,128)S(1)}, u32[]{:S(2)}, u32[]{:S(2)}) async-start(f32[4,64,128]{2,1,0:T(8,128)} %bitcast.73), calls=%async_computation.5 | async-start | bytes 262144 | tf_op jit(solution)/shard_map/all_to_all | solution.py:104
  85.8 17.9 %all-to-all-start.4 = ((f32[4,64,1024]{2,1,0:T(8,128)}), f32[4,64,1024]{2,1,0:T(8,128)S(1)}, u32[]{:S(2)}, u32[]{:S(2)}) async-start(f32[4,64,1024]{2,1,0:T(8,128)} %all_to_all.102), calls=%async_computation.4 | async-start | bytes 2097152 | tf_op jit(solution)/shard_map/all_to_all | solution.py:101
  (3 other events, 19.9 us)
